TPU v7x, 128 devices: a whole 4x4x4 slice. The times are simulated.
128 devices in a mesh: shard: 16 (over z, x), context: 4 (over y), tensor: 2 (over core).
Axes of the slice: x: 4, y: 4, z: 4, core: 2. Of those that a mesh axis runs over, the one named last changes fastest.
Arguments:
- inputs: float32 [32, 512, 768], P('shard', 'context'), may hold values from -6 to 6
- segment_ids: int32 [32, 512], P('shard', 'context'), may hold values from 0 to 3, never falling along the last dimension, each value on 1 to 256 neighbouring positions
- projection: bfloat16 [2, 3, 768, 768], P(None, None, 'shard', 'tensor'), may hold values from -1 to 1
- head_bias: bfloat16 [2, 2, 12, 64], P(None, None, 'tensor', 'shard'), may hold values from -3 to 3
- mixing: bfloat16 [2, 768, 768], P(None, 'tensor', 'shard'), may hold values from -0.875 to 0.875
- expansion: bfloat16 [2, 768, 3072], P(None, 'shard', 'tensor'), may hold values from -0.21875 to 0.21875
- hidden_bias: bfloat16 [2, 48, 64], P(None, 'tensor', 'shard'), may hold values from -3 to 3
- contraction: bfloat16 [2, 3072, 768], P(None, 'tensor', 'shard'), may hold values from -0.109375 to 0.109375
- norm_gains: bfloat16 [2, 2, 768], P(None, None, 'shard'), may hold values from 0.3984375 to 1.59375
- offsets: bfloat16 [2, 4, 768], P(None, None, 'shard'), may hold values from -2 to 2
- cotangent: float32 [32, 512, 768], P('shard', 'context'), may hold values from -6 to 6
Outputs:
- outputs: float32 [32, 512, 768], P('shard', 'context')
- input_grad: float32 [32, 512, 768], P('shard', 'context')
- grad_projection: float32 [2, 3, 768, 768], P(None, None, 'shard', 'tensor')
- head_grad: float32 [2, 2, 12, 64], P(None, None, 'tensor', 'shard')
- grad_mixing: float32 [2, 768, 768], P(None, 'tensor', 'shard')
- grad_expansion: float32 [2, 768, 3072], P(None, 'shard', 'tensor')
- hidden_grad: float32 [2, 48, 64], P(None, 'tensor', 'shard')
- grad_contraction: float32 [2, 3072, 768], P(None, 'tensor', 'shard')
- gains_grad: float32 [2, 2, 768], P(None, None, 'shard')
- grad_offsets: float32 [2, 4, 768], P(None, None, 'shard')
Inputs may be any that keep to these rules, and one draw needn't show every extreme that they name: `segment_ids`: within a row ids never fall; every document holds 1 to 256 positions and in every row some document holds exactly 256.
All inputs are finite; a program needn't handle non-finite values.
Results may differ from a plain program's by a relative error of at most 0.033.
Values may be sent and summed in bfloat16 or wider, within the bound.
No kernel may reach another device: no remote copies, remote signals or barrier semaphores. Data moves between devices by JAX's collectives and lax.ppermute only.
A program may use at most 128 MiB of HBM per device.

v0:
```python
import jax
import jax.numpy as jnp
from jax import lax
from jax.sharding import PartitionSpec as P

HEAD = 64
EPS = 1e-05
GELU_COEF = 0.7978845608028654
GELU_CUBE = 0.044715
MASKED = -1e30


def gelu_value(preact):
    inner_arg = GELU_COEF * (preact + GELU_CUBE * preact * preact * preact)
    return 0.5 * preact * (1.0 + jnp.tanh(inner_arg))


def gelu_slope(preact):
    inner_arg = GELU_COEF * (preact + GELU_CUBE * preact * preact * preact)
    tanh_value = jnp.tanh(inner_arg)
    return 0.5 * (1.0 + tanh_value) + 0.5 * preact * (1.0 - tanh_value * tanh_value) * GELU_COEF * (
        1.0 + 3.0 * GELU_CUBE * preact * preact
    )


def norm_forward(stream):
    center = stream - jnp.mean(stream, axis=-1, keepdims=True)
    spread = lax.rsqrt(jnp.mean(center * center, axis=-1, keepdims=True) + EPS)
    return (center * spread, spread)


def norm_backward(upstream, normed, spread, gain_row):
    scaled = upstream * gain_row
    first_mean = jnp.mean(scaled, axis=-1, keepdims=True)
    second_mean = jnp.mean(scaled * normed, axis=-1, keepdims=True)
    return spread * (scaled - first_mean - normed * second_mean)


def masked_scores(query_block, key_block, visible, head_scale):
    scores = (
        jnp.einsum("rqhe,rkhe->rhqk", query_block, key_block, preferred_element_type=jnp.float32)
        * head_scale
    )
    return jnp.where(visible, scores, MASKED)


def per_device(
    inputs,
    segment_ids,
    projection,
    head_bias,
    mixing,
    expansion,
    hidden_bias,
    contraction,
    norm_gains,
    offsets,
    cotangent,
):
    layers = projection.shape[0]
    row_count, block_length, model_width = inputs.shape
    context_size = lax.axis_size("context")
    heads_here = head_bias.shape[2]
    head_scale = HEAD ** (-0.5)
    segment_half = segment_ids.astype(jnp.bfloat16)
    query_pos = lax.axis_index("context") * block_length + jnp.arange(block_length, dtype=jnp.int32)
    key_pos = jnp.arange(block_length * context_size, dtype=jnp.int32)
    stream = inputs
    kept_state = []
    for layer_index in range(layers):
        weights = (
            lax.all_gather(projection[layer_index], "shard", axis=1, tiled=True),
            lax.all_gather(head_bias[layer_index], "shard", axis=2, tiled=True),
            lax.all_gather(mixing[layer_index], "shard", axis=1, tiled=True),
            lax.all_gather(expansion[layer_index], "shard", axis=0, tiled=True),
            lax.all_gather(hidden_bias[layer_index], "shard", axis=1, tiled=True),
            lax.all_gather(contraction[layer_index], "shard", axis=1, tiled=True),
            lax.all_gather(norm_gains[layer_index], "shard", axis=1, tiled=True),
            lax.all_gather(offsets[layer_index], "shard", axis=1, tiled=True),
        )
        (
            qkv_weight,
            qkv_bias,
            out_weight,
            up_weight,
            up_bias,
            down_weight,
            gain_rows,
            offset_rows,
        ) = weights
        gain_float = gain_rows.astype(jnp.float32)
        offset_float = offset_rows.astype(jnp.float32)
        normed_one, spread_one = norm_forward(stream)
        attend_input = (normed_one * gain_float[0] + offset_float[0]).astype(jnp.bfloat16)
        projected = jnp.einsum(
            "rtd,jdc->jrtc", attend_input, qkv_weight, preferred_element_type=jnp.float32
        )
        bias_float = qkv_bias.astype(jnp.float32).reshape(2, -1)
        query_rows = (projected[0] + bias_float[0]).astype(jnp.bfloat16)
        key_rows = projected[1].astype(jnp.bfloat16)
        value_rows = (projected[2] + bias_float[1]).astype(jnp.bfloat16)
        keys_all, values_all, segments_all = (
            lax.all_gather(key_rows, "context", axis=1, tiled=True),
            lax.all_gather(value_rows, "context", axis=1, tiled=True),
            lax.all_gather(segment_half, "context", axis=1, tiled=True),
        )
        visible = (segments_all[:, None, :] == segment_half[:, :, None]) & (
            key_pos[None, None, :] <= query_pos[None, :, None]
        )
        visible = visible[:, None]
        query_block = query_rows.reshape(row_count, block_length, heads_here, HEAD)
        key_block = keys_all.reshape(row_count, -1, heads_here, HEAD)
        value_block = values_all.reshape(row_count, -1, heads_here, HEAD)
        masked = masked_scores(query_block, key_block, visible, head_scale)
        row_top = jnp.max(masked, axis=-1, keepdims=True)
        log_total = row_top + jnp.log(jnp.sum(jnp.exp(masked - row_top), axis=-1, keepdims=True))
        soft_half = jnp.exp(masked - log_total).astype(jnp.bfloat16)
        attended = (
            jnp.einsum(
                "rhqk,rkhe->rqhe", soft_half, value_block, preferred_element_type=jnp.float32
            )
            .astype(jnp.bfloat16)
            .reshape(row_count, block_length, -1)
        )
        attend_part = jnp.einsum(
            "rtc,cd->rtd", attended, out_weight, preferred_element_type=jnp.float32
        )
        middle = stream + lax.psum(attend_part, "tensor") + offset_float[2]
        normed_two, spread_two = norm_forward(middle)
        feed_input = (normed_two * gain_float[1] + offset_float[1]).astype(jnp.bfloat16)
        preact = jnp.einsum(
            "rtd,df->rtf", feed_input, up_weight, preferred_element_type=jnp.float32
        ) + up_bias.astype(jnp.float32).reshape(-1)
        activation = gelu_value(preact).astype(jnp.bfloat16)
        feed_part = jnp.einsum(
            "rtf,fd->rtd", activation, down_weight, preferred_element_type=jnp.float32
        )
        stream = middle + lax.psum(feed_part, "tensor") + offset_float[3]
        stored = ()
        kept_state.append(
            (
                stored,
                normed_one,
                spread_one,
                attend_input,
                query_block,
                key_block,
                value_block,
                visible,
                log_total,
                attended,
                normed_two,
                spread_two,
                feed_input,
                preact,
                activation,
            )
        )
    upstream = cotangent
    collected = []
    for layer_index in reversed(range(layers)):
        (
            stored,
            normed_one,
            spread_one,
            attend_input,
            query_block,
            key_block,
            value_block,
            visible,
            log_total,
            attended,
            normed_two,
            spread_two,
            feed_input,
            preact,
            activation,
        ) = kept_state[layer_index]
        current = (
            lax.all_gather(projection[layer_index], "shard", axis=1, tiled=True),
            lax.all_gather(head_bias[layer_index], "shard", axis=2, tiled=True),
            lax.all_gather(mixing[layer_index], "shard", axis=1, tiled=True),
            lax.all_gather(expansion[layer_index], "shard", axis=0, tiled=True),
            lax.all_gather(hidden_bias[layer_index], "shard", axis=1, tiled=True),
            lax.all_gather(contraction[layer_index], "shard", axis=1, tiled=True),
            lax.all_gather(norm_gains[layer_index], "shard", axis=1, tiled=True),
            lax.all_gather(offsets[layer_index], "shard", axis=1, tiled=True),
        )
        (
            qkv_weight,
            qkv_bias,
            out_weight,
            up_weight,
            up_bias,
            down_weight,
            gain_rows,
            offset_rows,
        ) = current
        gain_float = gain_rows.astype(jnp.float32)
        upstream_half = upstream.astype(jnp.bfloat16)
        contraction_part = jnp.einsum(
            "rtf,rtd->fd", activation, upstream_half, preferred_element_type=jnp.float32
        )
        offset_down = jnp.sum(upstream, axis=(0, 1))
        hidden_back = jnp.einsum(
            "rtd,fd->rtf", upstream_half, down_weight, preferred_element_type=jnp.float32
        ) * gelu_slope(preact)
        hidden_half = hidden_back.astype(jnp.bfloat16)
        hidden_part = jnp.sum(hidden_back, axis=(0, 1)).reshape(up_bias.shape)
        expansion_part = jnp.einsum(
            "rtd,rtf->df", feed_input, hidden_half, preferred_element_type=jnp.float32
        )
        feed_partial = jnp.einsum(
            "rtf,df->rtd", hidden_half, up_weight, preferred_element_type=jnp.float32
        )
        feed_back = lax.psum(feed_partial.astype(jnp.bfloat16), "tensor").astype(jnp.float32)
        gain_two = jnp.sum(feed_back * normed_two, axis=(0, 1))
        offset_two = jnp.sum(feed_back, axis=(0, 1))
        middle_back = upstream + norm_backward(feed_back, normed_two, spread_two, gain_float[1])
        middle_half = middle_back.astype(jnp.bfloat16)
        mixing_part = jnp.einsum(
            "rtc,rtd->cd", attended, middle_half, preferred_element_type=jnp.float32
        )
        offset_mix = jnp.sum(middle_back, axis=(0, 1))
        attended_back = jnp.einsum(
            "rtd,cd->rtc", middle_half, out_weight, preferred_element_type=jnp.float32
        ).astype(jnp.bfloat16)
        back_heads = attended_back.reshape(row_count, block_length, heads_here, HEAD)
        attended_heads = attended.reshape(row_count, block_length, heads_here, HEAD)
        row_delta = jnp.sum(
            back_heads.astype(jnp.float32) * attended_heads.astype(jnp.float32), axis=-1
        )
        masked = masked_scores(query_block, key_block, visible, head_scale)
        soft = jnp.exp(masked - log_total)
        soft_half = soft.astype(jnp.bfloat16)
        prob_back = jnp.einsum(
            "rqhe,rkhe->rhqk", back_heads, value_block, preferred_element_type=jnp.float32
        )
        score_back = (
            soft * (prob_back - jnp.transpose(row_delta, (0, 2, 1))[..., None]) * head_scale
        ).astype(jnp.bfloat16)
        query_back = jnp.einsum(
            "rhqk,rkhe->rqhe", score_back, key_block, preferred_element_type=jnp.float32
        ).reshape(row_count, block_length, -1)
        key_full = jnp.einsum(
            "rhqk,rqhe->rkhe", score_back, query_block, preferred_element_type=jnp.float32
        ).reshape(row_count, block_length * context_size, -1)
        value_full = jnp.einsum(
            "rhqk,rqhe->rkhe", soft_half, back_heads, preferred_element_type=jnp.float32
        ).reshape(row_count, block_length * context_size, -1)
        key_back, value_back = (
            lax.psum_scatter(
                key_full.astype(jnp.bfloat16), "context", scatter_dimension=1, tiled=True
            ).astype(jnp.float32),
            lax.psum_scatter(
                value_full.astype(jnp.bfloat16), "context", scatter_dimension=1, tiled=True
            ).astype(jnp.float32),
        )
        head_part = jnp.stack(
            [jnp.sum(query_back, axis=(0, 1)), jnp.sum(value_back, axis=(0, 1))]
        ).reshape(qkv_bias.shape)
        project_back = jnp.stack([query_back, key_back, value_back]).astype(jnp.bfloat16)
        projection_part = jnp.einsum(
            "rtd,jrtc->jdc", attend_input, project_back, preferred_element_type=jnp.float32
        )
        input_partial = jnp.einsum(
            "jrtc,jdc->rtd", project_back, qkv_weight, preferred_element_type=jnp.float32
        )
        input_back = lax.psum(input_partial.astype(jnp.bfloat16), "tensor").astype(jnp.float32)
        gain_one = jnp.sum(input_back * normed_one, axis=(0, 1))
        offset_one = jnp.sum(input_back, axis=(0, 1))
        upstream = middle_back + norm_backward(input_back, normed_one, spread_one, gain_float[0])
        grad_parts = (
            projection_part,
            head_part,
            mixing_part,
            expansion_part,
            hidden_part,
            contraction_part,
            jnp.stack([gain_one, gain_two]),
            jnp.stack([offset_one, offset_two, offset_mix, offset_down]),
        )
        collected.insert(
            0,
            (
                lax.psum(
                    lax.psum_scatter(
                        grad_parts[0].astype(jnp.bfloat16), "shard", scatter_dimension=1, tiled=True
                    ),
                    "context",
                ).astype(jnp.float32),
                lax.psum(
                    lax.psum_scatter(
                        grad_parts[1].astype(jnp.bfloat16), "shard", scatter_dimension=2, tiled=True
                    ),
                    "context",
                ).astype(jnp.float32),
                lax.psum(
                    lax.psum_scatter(
                        grad_parts[2].astype(jnp.bfloat16), "shard", scatter_dimension=1, tiled=True
                    ),
                    "context",
                ).astype(jnp.float32),
                lax.psum(
                    lax.psum_scatter(
                        grad_parts[3].astype(jnp.bfloat16), "shard", scatter_dimension=0, tiled=True
                    ),
                    "context",
                ).astype(jnp.float32),
                lax.psum(
                    lax.psum_scatter(
                        grad_parts[4].astype(jnp.bfloat16), "shard", scatter_dimension=1, tiled=True
                    ),
                    "context",
                ).astype(jnp.float32),
                lax.psum(
                    lax.psum_scatter(
                        grad_parts[5].astype(jnp.bfloat16), "shard", scatter_dimension=1, tiled=True
                    ),
                    "context",
                ).astype(jnp.float32),
                lax.psum(
                    lax.psum_scatter(
                        grad_parts[6].astype(jnp.bfloat16), "shard", scatter_dimension=1, tiled=True
                    ),
                    "context",
                ).astype(jnp.float32),
                lax.psum(
                    lax.psum_scatter(
                        grad_parts[7].astype(jnp.bfloat16), "shard", scatter_dimension=1, tiled=True
                    ),
                    "context",
                ).astype(jnp.float32),
            ),
        )
    stacked = [jnp.stack([entry[member] for entry in collected]) for member in range(8)]
    return (
        stream,
        upstream,
        stacked[0],
        stacked[1],
        stacked[2],
        stacked[3],
        stacked[4],
        stacked[5],
        stacked[6],
        stacked[7],
    )


def solution(mesh):
    in_specs = (
        P("shard", "context", None),
        P("shard", "context"),
        P(None, None, "shard", "tensor"),
        P(None, None, "tensor", "shard"),
        P(None, "tensor", "shard"),
        P(None, "shard", "tensor"),
        P(None, "tensor", "shard"),
        P(None, "tensor", "shard"),
        P(None, None, "shard"),
        P(None, None, "shard"),
        P("shard", "context", None),
    )
    out_specs = (
        P("shard", "context", None),
        P("shard", "context", None),
        P(None, None, "shard", "tensor"),
        P(None, None, "tensor", "shard"),
        P(None, "tensor", "shard"),
        P(None, "shard", "tensor"),
        P(None, "tensor", "shard"),
        P(None, "tensor", "shard"),
        P(None, None, "shard"),
        P(None, None, "shard"),
    )
    return jax.shard_map(
        per_device, mesh=mesh, in_specs=in_specs, out_specs=out_specs, check_vma=False
    )
```

profile of v0, /device:TPU:0, one launch (start us, length us, event | category | flops | bytes accessed | tf_op | source)
XLA Modules:
  0.0 1538.7 jit_solution(7133893320823804238)
XLA Ops:
  10.4 25.5 %all-gather.1 = bf16[1,4,768]{1,0,2:T(2,128)(2,1)S(1)} all-gather(bf16[1,4,48]{1,0,2:T(2,128)(2,1)S(1)} %copy.288), channel_id=3, replica_groups=mesh['shard'=16,'context'=4,'tensor'=2] {'shard'}, dimensions={2}, use_global_device_ids=true | all-gather | bytes 6528 | tf_op jit(solution)/shard_map/all_gather | solution.py:79
  37.0 23.4 %all-gather = bf16[1,2,768]{1,0,2:T(2,128)(2,1)S(1)} all-gather(bf16[1,2,48]{1,0,2:T(2,128)(2,1)S(1)} %copy.287), channel_id=2, replica_groups=mesh['shard'=16,'context'=4,'tensor'=2] {'shard'}, dimensions={2}, use_global_device_ids=true | all-gather | bytes 3264 | tf_op jit(solution)/shard_map/all_gather | solution.py:78
  61.4 21.3 %all-gather.3 = bf16[1,2,6,64]{2,1,0,3:T(2,128)(2,1)S(1)} all-gather(bf16[1,2,6,4]{2,1,0,3:T(2,128)(2,1)S(1)} %copy.289), channel_id=5, replica_groups=mesh['shard'=16,'context'=4,'tensor'=2] {'shard'}, dimensions={3}, use_global_device_ids=true | all-gather | bytes 1632 | tf_op jit(solution)/shard_map/all_gather | solution.py:73
  83.1 10.0 all_gather.79
  93.1 23.9 %all-gather.5 = bf16[1,384,768]{1,2,0:T(8,128)(2,1)S(1)} all-gather(bf16[1,384,48]{1,2,0:T(8,128)(2,1)S(1)} %get-tuple-element.105), channel_id=7, replica_groups=mesh['shard'=16,'context'=4,'tensor'=2] {'shard'}, dimensions={2}, use_global_device_ids=true | all-gather | bytes 626688 | tf_op jit(solution)/shard_map/all_gather | solution.py:74
  117.2 4.6 slice_reduce_fusion.8
  122.1 11.0 slice_reduce_fusion.6
  136.3 14.4 all-gather.4
  157.9 13.3 all_gather.78
  178.3 21.3 %all-gather.7 = bf16[1,24,64]{1,0,2:T(2,128)(2,1)S(1)} all-gather(bf16[1,24,4]{1,0,2:T(2,128)(2,1)S(1)} %copy.290), channel_id=9, replica_groups=mesh['shard'=16,'context'=4,'tensor'=2] {'shard'}, dimensions={2}, use_global_device_ids=true | all-gather | bytes 3264 | tf_op jit(solution)/shard_map/all_gather | solution.py:76
  201.3 47.0 %all-gather.27.cloned.1.call-done = bf16[1,768,1536]{2,1,0:T(8,128)(2,1)} async-done(((bf16[1,48,1536]{2,1,0:T(8,128)(2,1)}), bf16[1,768,1536]{2,1,0:T(8,128)(2,1)}) %all-gather.27.cloned.1.call-update) | async-done | bytes 2359312 | tf_op jit(solution)/shard_map/all_gather | solution.py:75
  250.9 45.3 %all-gather.29.cloned.1.call-done = bf16[1,1536,768]{1,2,0:T(8,128)(2,1)} async-done(((bf16[1,1536,48]{1,2,0:T(8,128)(2,1)}), bf16[1,1536,768]{1,2,0:T(8,128)(2,1)}) %all-gather.29.cloned.1.call-update) | async-done | bytes 2359312 | tf_op jit(solution)/shard_map/all_gather | solution.py:77
  300.7 23.3 %all-gather.10 = bf16[1,4,768]{1,0,2:T(2,128)(2,1)S(1)} all-gather(bf16[1,4,48]{1,0,2:T(2,128)(2,1)S(1)} %copy.292), channel_id=12, replica_groups=mesh['shard'=16,'context'=4,'tensor'=2] {'shard'}, dimensions={2}, use_global_device_ids=true | all-gather | bytes 6528 | tf_op jit(solution)/shard_map/all_gather | solution.py:79
  324.5 22.4 %all-gather.9 = bf16[1,2,768]{1,0,2:T(2,128)(2,1)S(1)} all-gather(bf16[1,2,48]{1,0,2:T(2,128)(2,1)S(1)} %copy.291), channel_id=11, replica_groups=mesh['shard'=16,'context'=4,'tensor'=2] {'shard'}, dimensions={2}, use_global_device_ids=true | all-gather | bytes 3264 | tf_op jit(solution)/shard_map/all_gather | solution.py:78
  347.3 22.1 %all-gather.12 = bf16[1,2,6,64]{2,1,0,3:T(2,128)(2,1)S(1)} all-gather(bf16[1,2,6,4]{2,1,0,3:T(2,128)(2,1)S(1)} %copy.293), channel_id=14, replica_groups=mesh['shard'=16,'context'=4,'tensor'=2] {'shard'}, dimensions={3}, use_global_device_ids=true | all-gather | bytes 1632 | tf_op jit(solution)/shard_map/all_gather | solution.py:73
  370.8 24.5 %all-gather.14 = bf16[1,384,768]{1,2,0:T(8,128)(2,1)} all-gather(bf16[1,384,48]{1,2,0:T(8,128)(2,1)S(1)} %get-tuple-element.104), channel_id=16, replica_groups=mesh['shard'=16,'context'=4,'tensor'=2] {'shard'}, dimensions={2}, use_global_device_ids=true | all-gather | bytes 626688 | tf_op jit(solution)/shard_map/all_gather | solution.py:74
  395.4 4.6 slice_reduce_fusion.2
  400.0 11.2 slice_reduce_fusion
  416.2 15.3 all-gather.13
  438.4 14.1 all_gather.89
  460.8 22.6 %all-gather.16 = bf16[1,24,64]{1,0,2:T(2,128)(2,1)S(1)} all-gather(bf16[1,24,4]{1,0,2:T(2,128)(2,1)S(1)} %copy.294), channel_id=18, replica_groups=mesh['shard'=16,'context'=4,'tensor'=2] {'shard'}, dimensions={2}, use_global_device_ids=true | all-gather | bytes 3264 | tf_op jit(solution)/shard_map/all_gather | solution.py:76
  486.8 44.9 %all-gather.33.cloned.1.call-done = bf16[1,768,1536]{2,1,0:T(8,128)(2,1)} async-done(((bf16[1,48,1536]{2,1,0:T(8,128)(2,1)}), bf16[1,768,1536]{2,1,0:T(8,128)(2,1)}) %all-gather.33.cloned.1.call-update) | async-done | bytes 2359312 | tf_op jit(solution)/shard_map/all_gather | solution.py:75
  531.7 3.7 convolution_add_fusion
  535.4 43.8 %all-gather.35.cloned.1.call-done = bf16[1,1536,768]{1,2,0:T(8,128)(2,1)} async-done(((bf16[1,1536,48]{1,2,0:T(8,128)(2,1)}), bf16[1,1536,768]{1,2,0:T(8,128)(2,1)}) %all-gather.35.cloned.1.call-update) | async-done | bytes 2359312 | tf_op jit(solution)/shard_map/all_gather | solution.py:77
  579.1 4.5 fusion.157
  586.1 4.1 fusion.3
  590.5 19.0 %all-reduce.36.cloned.1.call-done = bf16[2,128,768]{2,1,0:T(8,128)(2,1)} async-done(((bf16[2,128,768]{2,1,0:T(8,128)(2,1)}), bf16[2,128,768]{2,1,0:T(8,128)(2,1)}) %all-reduce.36.cloned.1.call-update) | async-done | bytes 393232 | tf_op jit(solution)/shard_map/psum | solution.py:216
  612.0 26.7 %all-reduce.34.cloned.1.call-done = f32[2,128,768]{2,1,0:T(8,128)} async-done(((f32[2,128,768]{2,1,0:T(8,128)}), f32[2,128,768]{2,1,0:T(8,128)}) %all-reduce.34.cloned.1.call-update) | async-done | bytes 786448 | tf_op jit(solution)/shard_map/psum | solution.py:138
  655.3 3.8 convolution_convert_fusion.2
  664.7 14.6 reduce-scatter.21.cloned.1.call-done
  679.2 24.7 %reduce-scatter.23.cloned.1.call-done = bf16[2,128,384]{2,1,0:T(8,128)(2,1)} async-done(((bf16[2,512,384]{2,1,0:T(8,128)(2,1)}), bf16[2,128,384]{2,1,0:T(8,128)(2,1)}) %reduce-scatter.23.cloned.1.call-update) | async-done | bytes 196624 | tf_op jit(solution)/shard_map/reduce_scatter | solution.py:255
  707.3 24.0 %all-reduce.38.cloned.1.call-done = bf16[2,128,768]{2,1,0:T(8,128)(2,1)} async-done(((bf16[2,128,768]{2,1,0:T(8,128)(2,1)}), bf16[2,128,768]{2,1,0:T(8,128)(2,1)}) %all-reduce.38.cloned.1.call-update) | async-done | bytes 393232 | tf_op jit(solution)/shard_map/psum | solution.py:269
  738.9 25.5 %all-reduce.40.cloned.1.call-done = bf16[2,128,768]{2,1,0:T(8,128)(2,1)} async-done(((bf16[2,128,768]{2,1,0:T(8,128)(2,1)}), bf16[2,128,768]{2,1,0:T(8,128)(2,1)}) %all-reduce.40.cloned.1.call-update) | async-done | bytes 393232 | tf_op jit(solution)/shard_map/psum | solution.py:216
  780.8 3.9 convolution_convert_fusion
  791.8 12.8 reduce-scatter.25.cloned.1.call-done
  804.6 24.5 %reduce-scatter.27.cloned.1.call-done = bf16[2,128,384]{2,1,0:T(8,128)(2,1)} async-done(((bf16[2,512,384]{2,1,0:T(8,128)(2,1)}), bf16[2,128,384]{2,1,0:T(8,128)(2,1)}) %reduce-scatter.27.cloned.1.call-update) | async-done | bytes 196624 | tf_op jit(solution)/shard_map/reduce_scatter | solution.py:255
  840.5 5.3 copy.244
  847.9 5.2 copy.242
  857.7 3.9 bitcast_convert_fusion
  875.5 75.6 %all-reduce.12 = (bf16[2,6,64]{1,0,2:T(2,128)(2,1)S(1)}, bf16[2,6,64]{1,0,2:T(2,128)(2,1)S(1)}, bf16[24,64]{1,0:T(8,128)(2,1)S(1)}, bf16[24,64]{1,0:T(8,128)(2,1...) all-reduce(bf16[2,6,64]{1,0,2:T(2,128)(2,1)S(1)} %copy.249, ...), channel_id=27, replica_groups=mesh['shard'=16,'context'=4,'tensor'=2] {'shard'}, use_global_device_ids=true, to_apply=%region_44.45.clone | all-reduce | flops 13824 | bytes 55296
  956.3 52.0 %reduce-scatter.37.cloned.1.call-done = bf16[384,48]{0,1:T(8,128)(2,1)} async-done(((bf16[384,768]{0,1:T(8,128)(2,1)}), bf16[384,48]{0,1:T(8,128)(2,1)}) %reduce-scatter.37.cloned.1.call-update) | async-done | bytes 36880
  1008.4 111.1 %all-reduce.44.cloned.1.call-done = (bf16[3,768,384]{2,0,1:T(4,128)(2,1)}, bf16[3,768,384]{2,0,1:T(4,128)(2,1)}) async-done(((bf16[3,768,384]{2,0,1:T(4,128)(2,1)}, bf16[3,768,384]{2,0,1:T(4,128)(2,1)}), (bf16[3,768,384]{2,0,1:T(4,128)(2,1)}, bf16[3,768,384]{2,0,1:T(4,128)(2,1)})) %all-reduce.44.cloned.1.call-update) | async-done | bytes 3538960
  1122.7 75.1 %reduce-scatter.31.cloned.1.call-done = bf16[48,1536]{1,0:T(8,128)(2,1)} async-done(((bf16[768,1536]{1,0:T(8,128)(2,1)}), bf16[48,1536]{1,0:T(8,128)(2,1)}) %reduce-scatter.31.cloned.1.call-update) | async-done | bytes 147472 | tf_op jit(solution)/shard_map/reduce_scatter | solution.py:305
  1197.8 77.9 %reduce-scatter.35.cloned.1.call-done = bf16[1536,48]{0,1:T(8,128)(2,1)} async-done(((bf16[1536,768]{0,1:T(8,128)(2,1)}), bf16[1536,48]{0,1:T(8,128)(2,1)}) %reduce-scatter.35.cloned.1.call-update) | async-done | bytes 147472 | tf_op jit(solution)/shard_map/reduce_scatter | solution.py:317
  1275.7 77.7 %reduce-scatter.29.cloned.1.call-done = bf16[48,1536]{1,0:T(8,128)(2,1)} async-done(((bf16[768,1536]{1,0:T(8,128)(2,1)}), bf16[48,1536]{1,0:T(8,128)(2,1)}) %reduce-scatter.29.cloned.1.call-update) | async-done | bytes 147472 | tf_op jit(solution)/shard_map/reduce_scatter | solution.py:305
  1353.3 77.9 %reduce-scatter.33.cloned.1.call-done = bf16[1536,48]{0,1:T(8,128)(2,1)} async-done(((bf16[1536,768]{0,1:T(8,128)(2,1)}), bf16[1536,48]{0,1:T(8,128)(2,1)}) %reduce-scatter.33.cloned.1.call-update) | async-done | bytes 147472 | tf_op jit(solution)/shard_map/reduce_scatter | solution.py:317
  1432.5 43.3 %all-reduce.46.cloned.1.call-done = (bf16[1,2,6,4]{2,3,1,0:T(4,128)(2,1)}, bf16[1,2,6,4]{2,3,1,0:T(4,128)(2,1)}, bf16[1,384,48]{1,2,0:T(8,128)(2,1)}, bf16[1,384...) async-done(((bf16[1,2,6,4]{2,3,1,0:T(4,128)(2,1)}, ...) | async-done | bytes 75472 | tf_op jit(solution)/shard_map/psum | solution.py:292
  1482.4 42.9 %all-reduce.48.cloned.1.call-done = (bf16[1,3,48,384]{3,1,2,0:T(4,128)(2,1)}, bf16[1,3,48,384]{3,1,2,0:T(4,128)(2,1)}, bf16[1,48,1536]{2,1,0:T(8,128)(2,1)}, bf1...) async-done(((bf16[1,3,48,384]{3,1,2,0:T(4,128)(2,1)}, bf16[1,3,48,384]{3,1,2,0:T(4,128)(2,1)}, bf16[1,48,1536]{2,1,0:T(8,128)(2,1)}, ...) | async-done | bytes 811024 | tf_op jit(solution)/shard_map/psum | solution.py:286
  (425 shorter events, 172.3 us)
Async XLA Ops:
  7.2 29.1 %copy-start.83 = (bf16[2,2,48]{2,1,0:T(2,128)(2,1)S(1)}, bf16[2,2,48]{2,1,0:T(2,128)(2,1)}, u32[]{:S(2)}) copy-start(bf16[2,2,48]{2,1,0:T(2,128)(2,1)} %param.19) | copy-start | bytes 1156
  7.2 53.6 %copy-start.88 = (s32[2,128]{1,0:T(2,128)S(1)}, s32[2,128]{1,0:T(2,128)}, u32[]{:S(2)}) copy-start(s32[2,128]{1,0:T(2,128)} %param.12) | copy-start | bytes 3076
  7.2 53.6 %copy-start.76 = (bf16[2,2,6,4]{2,3,1,0:T(4,128)(2,1)S(1)}, bf16[2,2,6,4]{2,3,1,0:T(4,128)(2,1)}, u32[]{:S(2)}) copy-start(bf16[2,2,6,4]{2,3,1,0:T(4,128)(2,1)} %param.14) | copy-start | bytes 580
  7.2 75.7 %copy-start = (f32[2,128,768]{2,1,0:T(8,128)S(1)}, f32[2,128,768]{2,1,0:T(8,128)}, u32[]{:S(2)}) copy-start(f32[2,128,768]{2,1,0:T(8,128)} %param.11) | copy-start | bytes 2359300
  7.2 126.0 %all-gather.25.cloned.1.call-start = ((), (), s32[]{:S(2)}) async-start(), calls=%async_computation.26 | async-start | bytes 1880064 | tf_op jit(solution)/shard_map/all_gather | solution.py:72
  9.0 84.1 %copy-start.41 = (bf16[2,384,48]{1,2,0:T(8,128)(2,1)S(1)}, bf16[2,384,48]{1,2,0:T(8,128)(2,1)}, u32[]{:S(2)}) copy-start(bf16[2,384,48]{1,2,0:T(8,128)(2,1)} %param.15) | copy-start | bytes 221188
  9.0 190.7 %all-reduce.28.cloned.1.call-start = ((), (), s32[]{:S(2)}) async-start(), calls=%async_computation.10 | async-start | bytes 1572864 | tf_op jit(solution)/shard_map/psum | solution.py:128
  82.8 71.6 %copy-start.50 = (f32[6,64]{1,0:T(8,128)}, f32[6,64]{1,0:T(8,128)S(1)}, u32[]{:S(2)}) copy-start(f32[6,64]{1,0:T(8,128)S(1)} %copy.213) | copy-start | bytes 4612
  117.0 57.7 %copy-start.10 = (bf16[1,384,768]{1,2,0:T(8,128)(2,1)}, bf16[1,384,768]{1,2,0:T(8,128)(2,1)S(1)}, u32[]{:S(2)}) copy-start(bf16[1,384,768]{1,2,0:T(8,128)(2,1)S(1)} %all-gather.5) | copy-start | bytes 1769476
  122.1 49.4 %copy-start.20 = (pred[2,128,512]{2,1,0:T(8,128)(4,1)}, pred[2,128,512]{2,1,0:T(8,128)(4,1)S(1)}, u32[]{:S(2)}) copy-start(pred[2,128,512]{2,1,0:T(8,128)(4,1)S(1)} %compare_and_fusion) | copy-start | bytes 393220
  133.2 115.2 %copy-start.61 = (f32[768]{0:T(1024)}, f32[768]{0:T(1024)S(1)}, u32[]{:S(2)}) copy-start(f32[768]{0:T(1024)S(1)} %get-tuple-element.49) | copy-start | bytes 9220
  176.1 72.3 %all-gather.27.cloned.1.call-start = ((), (), s32[]{:S(2)}) async-start(), calls=%async_computation.27 | async-start | bytes 2506752 | tf_op jit(solution)/shard_map/all_gather | solution.py:75
  176.9 119.4 %all-gather.29.cloned.1.call-start = ((), (), s32[]{:S(2)}) async-start(), calls=%async_computation.28 | async-start | bytes 2506752 | tf_op jit(solution)/shard_map/all_gather | solution.py:77
  177.7 233.5 %all-reduce.30.cloned.1.call-start = ((), (), s32[]{:S(2)}) async-start(), calls=%async_computation.11 | async-start | bytes 1572864 | tf_op jit(solution)/shard_map/psum | solution.py:138
  201.1 49.8 %copy-start.55 = (f32[2,128]{1,0:T(2,128)}, f32[2,128]{1,0:T(2,128)S(1)}, u32[]{:S(2)}) copy-start(f32[2,128]{1,0:T(2,128)S(1)} %broadcast_multiply_fusion.10) | copy-start | bytes 3076
  201.3 49.6 %copy-start.64 = (f32[2,128]{1,0:T(2,128)}, f32[2,128]{1,0:T(2,128)S(1)}, u32[]{:S(2)}) copy-start(f32[2,128]{1,0:T(2,128)S(1)} %add_rsqrt_fusion.2) | copy-start | bytes 3076
  250.9 45.3 %copy-start.90 = (f32[2,128,1536]{2,1,0:T(8,128)}, f32[2,128,1536]{2,1,0:T(8,128)S(1)}, u32[]{:S(2)}) copy-start(f32[2,128,1536]{2,1,0:T(8,128)S(1)} %convolution_add_fusion.1) | copy-start | bytes 4718596
  250.9 49.6 %copy-start.79 = (bf16[1,4,48]{2,1,0:T(4,128)(2,1)S(1)}, bf16[1,4,48]{2,1,0:T(4,128)(2,1)}, u32[]{:S(2)}) copy-start(bf16[1,4,48]{2,1,0:T(4,128)(2,1)} %get-tuple-element.115) | copy-start | bytes 1156
  299.9 47.4 %copy-start.75 = (bf16[1,2,6,4]{2,3,1,0:T(4,128)(2,1)S(1)}, bf16[1,2,6,4]{2,3,1,0:T(4,128)(2,1)}, u32[]{:S(2)}) copy-start(bf16[1,2,6,4]{2,3,1,0:T(4,128)(2,1)} %get-tuple-element.110) | copy-start | bytes 292
  299.9 112.8 %all-gather.31.cloned.1.call-start = ((), (), s32[]{:S(2)}) async-start(), calls=%async_computation.29 | async-start | bytes 1880064 | tf_op jit(solution)/shard_map/all_gather | solution.py:72
  300.5 183.7 %all-reduce.32.cloned.1.call-start = ((), (), s32[]{:S(2)}) async-start(), calls=%async_computation.12 | async-start | bytes 1572864 | tf_op jit(solution)/shard_map/psum | solution.py:128
  457.9 26.3 %copy-start.28 = (bf16[2,6,64,128]{3,2,1,0:T(8,128)(2,1)}, bf16[2,6,64,128]{3,2,1,0:T(8,128)(2,1)S(1)}, u32[]{:S(2)}) copy-start(bf16[2,6,64,128]{3,2,1,0:T(8,128)(2,1)S(1)} %convolution_convert_fusion.4) | copy-start | bytes 589828
  459.3 72.4 %all-gather.33.cloned.1.call-start = ((), (), s32[]{:S(2)}) async-start(), calls=%async_computation.30 | async-start | bytes 2506752 | tf_op jit(solution)/shard_map/all_gather | solution.py:75
  460.0 119.1 %all-gather.35.cloned.1.call-start = ((), (), s32[]{:S(2)}) async-start(), calls=%async_computation.31 | async-start | bytes 2506752 | tf_op jit(solution)/shard_map/all_gather | solution.py:77
  460.7 148.8 %all-reduce.36.cloned.1.call-start = ((), (), s32[]{:S(2)}) async-start(), calls=%async_computation.14 | async-start | bytes 786432 | tf_op jit(solution)/shard_map/psum | solution.py:216
  586.1 52.6 %all-reduce.34.cloned.1.call-start = ((), (), s32[]{:S(2)}) async-start(), calls=%async_computation.13 | async-start | bytes 1572864 | tf_op jit(solution)/shard_map/psum | solution.py:138
  590.2 89.0 %reduce-scatter.21.cloned.1.call-start = ((), (), s32[]{:S(2)}) async-start(), calls=%async_computation.15 | async-start | bytes 983040 | tf_op jit(solution)/shard_map/reduce_scatter | solution.py:252
  655.2 48.7 %reduce-scatter.23.cloned.1.call-start = ((), (), s32[]{:S(2)}) async-start(), calls=%async_computation.16 | async-start | bytes 983040 | tf_op jit(solution)/shard_map/reduce_scatter | solution.py:255
  661.4 69.9 %all-reduce.38.cloned.1.call-start = ((), (), s32[]{:S(2)}) async-start(), calls=%async_computation.17 | async-start | bytes 786432 | tf_op jit(solution)/shard_map/psum | solution.py:269
  704.0 27.3 %copy-start.49 = (f32[2,128]{1,0:T(2,128)S(1)}, f32[2,128]{1,0:T(2,128)}, u32[]{:S(2)}) copy-start(f32[2,128]{1,0:T(2,128)} %copy-done.48) | copy-start | bytes 3076
  704.0 27.3 %copy-start.58 = (f32[2,128]{1,0:T(2,128)S(1)}, f32[2,128]{1,0:T(2,128)}, u32[]{:S(2)}) copy-start(f32[2,128]{1,0:T(2,128)} %copy-done.57) | copy-start | bytes 3076
  707.2 57.2 %all-reduce.40.cloned.1.call-start = ((), (), s32[]{:S(2)}) async-start(), calls=%async_computation.18 | async-start | bytes 786432 | tf_op jit(solution)/shard_map/psum | solution.py:216
  737.3 27.1 %copy-start.56 = (f32[2,128]{1,0:T(2,128)S(1)}, f32[2,128]{1,0:T(2,128)}, u32[]{:S(2)}) copy-start(f32[2,128]{1,0:T(2,128)} %copy-done.55) | copy-start | bytes 3076
  737.3 27.1 %copy-start.65 = (f32[2,128]{1,0:T(2,128)S(1)}, f32[2,128]{1,0:T(2,128)}, u32[]{:S(2)}) copy-start(f32[2,128]{1,0:T(2,128)} %copy-done.64) | copy-start | bytes 3076
  738.9 65.7 %reduce-scatter.25.cloned.1.call-start = ((), (), s32[]{:S(2)}) async-start(), calls=%async_computation.19 | async-start | bytes 983040 | tf_op jit(solution)/shard_map/reduce_scatter | solution.py:252
  780.5 48.5 %reduce-scatter.27.cloned.1.call-start = ((), (), s32[]{:S(2)}) async-start(), calls=%async_computation.20 | async-start | bytes 983040 | tf_op jit(solution)/shard_map/reduce_scatter | solution.py:255
  787.0 85.9 %all-reduce.42.cloned.1.call-start = ((), (), s32[]{:S(2)}) async-start(), calls=%async_computation.21 | async-start | bytes 786432 | tf_op jit(solution)/shard_map/psum | solution.py:269
  832.3 123.9 %reduce-scatter.39.cloned.1.call-start = ((), (), s32[]{:S(2)}) async-start(), calls=%async_computation.33 | async-start | bytes 626688
  834.9 173.4 %reduce-scatter.37.cloned.1.call-start = ((), (), s32[]{:S(2)}) async-start(), calls=%async_computation.32 | async-start | bytes 626688
  837.3 282.1 %all-reduce.44.cloned.1.call-start = ((), (), s32[]{:S(2)}) async-start(), calls=%async_computation.34 | async-start | bytes 9437184
  853.1 344.7 %reduce-scatter.31.cloned.1.call-start = ((), (), s32[]{:S(2)}) async-start(), calls=%async_computation.23 | async-start | bytes 2506752 | tf_op jit(solution)/shard_map/reduce_scatter | solution.py:305
  856.6 419.0 %reduce-scatter.35.cloned.1.call-start = ((), (), s32[]{:S(2)}) async-start(), calls=%async_computation.25 | async-start | bytes 2506752 | tf_op jit(solution)/shard_map/reduce_scatter | solution.py:317
  861.6 491.7 %reduce-scatter.29.cloned.1.call-start = ((), (), s32[]{:S(2)}) async-start(), calls=%async_computation.22 | async-start | bytes 2506752 | tf_op jit(solution)/shard_map/reduce_scatter | solution.py:305
  865.1 566.1 %reduce-scatter.33.cloned.1.call-start = ((), (), s32[]{:S(2)}) async-start(), calls=%async_computation.24 | async-start | bytes 2506752 | tf_op jit(solution)/shard_map/reduce_scatter | solution.py:317
  869.2 606.6 %all-reduce.46.cloned.1.call-start = ((), (), s32[]{:S(2)}) async-start(), calls=%async_computation.35 | async-start | bytes 165888 | tf_op jit(solution)/shard_map/psum | solution.py:292
  872.7 558.6 %copy-start.4 = (f32[2,128,768]{2,1,0:T(8,128)S(1)}, f32[2,128,768]{2,1,0:T(8,128)}, u32[]{:S(2)}) copy-start(f32[2,128,768]{2,1,0:T(8,128)} %copy-done.3) | copy-start | bytes 2359300
  872.9 558.4 %copy-start.19 = (bf16[2,128,768]{2,1,0:T(8,128)(2,1)S(1)}, bf16[2,128,768]{2,1,0:T(8,128)(2,1)}, u32[]{:S(2)}) copy-start(bf16[2,128,768]{2,1,0:T(8,128)(2,1)} %all-reduce.42.cloned.1.call-done) | copy-start | bytes 1179652
  1008.3 516.9 %all-reduce.48.cloned.1.call-start = ((), (), s32[]{:S(2)}) async-start(), calls=%async_computation.36 | async-start | bytes 1769472 | tf_op jit(solution)/shard_map/psum | solution.py:286
  (72 other events, 288.1 us)
Sparse Core Ops, SparseCore 0:
  10.8 47.1 all-gather.24
  176.2 21.9 all-reduce.27
  201.2 47.1 all-gather.26
  251.2 45.0 all-gather.28
  300.0 24.0 all-reduce.29
  326.1 46.5 all-gather.30
  459.4 22.1 all-reduce.31
  484.5 47.1 all-gather.32
  534.0 45.0 all-gather.34
  586.2 23.2 all-reduce.35
  612.5 26.1 all-reduce.33
  655.4 23.8 reduce-scatter.20
  681.8 22.1 reduce-scatter.22
  707.4 23.8 all-reduce.37
  739.0 25.3 all-reduce.39
  780.6 23.8 reduce-scatter.24
  806.9 22.0 reduce-scatter.26
  832.5 23.8 all-reduce.41
  860.1 73.2 reduce-scatter.38
  937.1 71.1 reduce-scatter.36
  1011.7 107.6 all-reduce.43
  1123.1 74.6 reduce-scatter.30
  1201.4 74.1 reduce-scatter.34
  1279.2 74.1 reduce-scatter.28
  1357.0 74.2 reduce-scatter.32
  1435.6 40.1 all-reduce.45
  1479.0 46.2 all-reduce.47
where the time goes:
time: 1540 us
  waiting for transfers between devices  913 us (59%)
  blocking collectives  373 us (24%)
  local copies, waits for them, and re-layouts  101 us (7%)
  matrix products  92.7 us (6%)
  other arithmetic  40.6 us (3%)
  between operations  17.3 us (1%)
    unnamed x30, waiting for transfers between devices  165 us
    reduce_scatter x2, waiting for transfers between devices, per_device(): lax.psum_scatter(grad_parts[5].astype(jnp.bfloat16), 'shard', scatter_dim...  156 us
    reduce_scatter x2, waiting for transfers between devices, per_device(): lax.psum_scatter(grad_parts[3].astype(jnp.bfloat16), 'shard', scatter_dim...  153 us
    all_gather x2, waiting for transfers between devices, per_device(): lax.all_gather(expansion[layer_index], 'shard', axis=0, tiled=True)  91.9 us
    all_gather x2, waiting for transfers between devices, per_device(): lax.all_gather(contraction[layer_index], 'shard', axis=1, tiled=True)  89.1 us
    unnamed x1, blocking collectives  75.6 us
    reduce_scatter x2, waiting for transfers between devices, per_device(): lax.psum_scatter(value_full.astype(jnp.bfloat16), 'context', scatter_dime...  49.3 us
    all_gather x2, blocking collectives, per_device(): lax.all_gather(offsets[layer_index], 'shard', axis=1, tiled=True)  48.7 us
  transfers between devices with their start and end apart: 27, of which 20 were waited for; matrix products, arithmetic and copies ran while one was open for 9% of the time, Pallas kernels for 0%

commit v1 on v0

--- a/solution.py
+++ b/solution.py
@@ -8,6 +8,12 @@
 GELU_COEF = 0.7978845608028654
 GELU_CUBE = 0.044715
 MASKED = -1e30
+
+
+def tiled_gather(x, axis, dim):
+    size = lax.axis_size(axis)
+    repeats = [size if d == dim else 1 for d in range(x.ndim)]
+    return lax.all_to_all(jnp.tile(x, repeats), axis, split_axis=dim, concat_axis=dim, tiled=True)
 
 
 def gelu_value(preact):
@@ -71,7 +77,7 @@
         weights = (
             lax.all_gather(projection[layer_index], "shard", axis=1, tiled=True),
             lax.all_gather(head_bias[layer_index], "shard", axis=2, tiled=True),
-            lax.all_gather(mixing[layer_index], "shard", axis=1, tiled=True),
+            tiled_gather(mixing[layer_index], "shard", 1),
             lax.all_gather(expansion[layer_index], "shard", axis=0, tiled=True),
             lax.all_gather(hidden_bias[layer_index], "shard", axis=1, tiled=True),
             lax.all_gather(contraction[layer_index], "shard", axis=1, tiled=True),

time: 1540 us -> 1520 us (0.987)
  waiting for transfers between devices: 913 us -> 860 us
    psum x2, waiting for transfers between devices: 44.5 us -> 0.01 us  [per_device(): lax.psum(feed_partial.astype(jnp.bfloat16), 'tensor').astype(jnp.float32)]
  transfers between devices with their start and end apart: 27 -> 29, of which waited for: 20 -> 18; matrix products, arithmetic and copies ran while one was open for 9% -> 11% of each run, Pallas kernels for 0% -> 0%
where the time goes in v1:
time: 1520 us; the launch traced here: 1510 us
  waiting for transfers between devices  860 us (57%)
  blocking collectives  381 us (25%)
  local copies, waits for them, and re-layouts  105 us (7%)
  matrix products  93.1 us (6%)
  other arithmetic  42.1 us (3%)
  between operations  17.3 us (1%)
    unnamed x30, waiting for transfers between devices  165 us
    reduce_scatter x2, waiting for transfers between devices, per_device(): lax.psum_scatter(grad_parts[5].astype(jnp.bfloat16), 'shard', scatter_dim...  156 us
    reduce_scatter x2, waiting for transfers between devices, per_device(): lax.psum_scatter(grad_parts[3].astype(jnp.bfloat16), 'shard', scatter_dim...  153 us
    all_gather x2, waiting for transfers between devices, per_device(): lax.all_gather(expansion[layer_index], 'shard', axis=0, tiled=True)  93.6 us
    all_gather x2, waiting for transfers between devices, per_device(): lax.all_gather(contraction[layer_index], 'shard', axis=1, tiled=True)  88 us
    unnamed x1, blocking collectives  75.5 us
    all_gather x2, blocking collectives, per_device(): lax.all_gather(offsets[layer_index], 'shard', axis=1, tiled=True)  53 us
    all_gather x2, blocking collectives, per_device(): lax.all_gather(mixing[layer_index], 'shard', axis=1, tiled=True)  52.7 us
  transfers between devices with their start and end apart: 29, of which 18 were waited for; matrix products, arithmetic and copies ran while one was open for 11% of the time, Pallas kernels for 0%

profile of v1, /device:TPU:0, one launch (start us, length us, event | category | flops | bytes accessed | tf_op | source)
XLA Modules:
  0.0 1512.7 jit_solution(6753785413496350685)
XLA Ops:
  11.2 8.1 all-to-all-start
  20.1 26.9 %all-gather.1 = bf16[1,4,768]{1,0,2:T(2,128)(2,1)S(1)} all-gather(bf16[1,4,48]{1,0,2:T(2,128)(2,1)S(1)} %copy.302), channel_id=3, replica_groups=mesh['shard'=16,'context'=4,'tensor'=2] {'shard'}, dimensions={2}, use_global_device_ids=true | all-gather | bytes 6528 | tf_op jit(solution)/shard_map/all_gather | solution.py:85
  48.0 22.0 %all-gather = bf16[1,2,768]{1,0,2:T(2,128)(2,1)S(1)} all-gather(bf16[1,2,48]{1,0,2:T(2,128)(2,1)S(1)} %copy.301), channel_id=2, replica_groups=mesh['shard'=16,'context'=4,'tensor'=2] {'shard'}, dimensions={2}, use_global_device_ids=true | all-gather | bytes 3264 | tf_op jit(solution)/shard_map/all_gather | solution.py:84
  70.5 22.3 %all-gather.3 = bf16[1,2,6,64]{2,1,0,3:T(2,128)(2,1)S(1)} all-gather(bf16[1,2,6,4]{2,1,0,3:T(2,128)(2,1)S(1)} %copy.303), channel_id=5, replica_groups=mesh['shard'=16,'context'=4,'tensor'=2] {'shard'}, dimensions={3}, use_global_device_ids=true | all-gather | bytes 1632 | tf_op jit(solution)/shard_map/all_gather | solution.py:79
  93.2 10.4 all_gather.77
  103.9 4.6 slice_reduce_fusion.8
  108.8 11.0 slice_reduce_fusion.6
  123.0 14.0 all-gather.4
  139.9 13.3 all_gather.76
  162.8 22.2 %all-gather.6 = bf16[1,24,64]{1,0,2:T(2,128)(2,1)S(1)} all-gather(bf16[1,24,4]{1,0,2:T(2,128)(2,1)S(1)} %copy.304), channel_id=8, replica_groups=mesh['shard'=16,'context'=4,'tensor'=2] {'shard'}, dimensions={2}, use_global_device_ids=true | all-gather | bytes 3264 | tf_op jit(solution)/shard_map/all_gather | solution.py:82
  186.8 46.4 %all-gather.27.cloned.1.call-done = bf16[1,768,1536]{2,1,0:T(8,128)(2,1)} async-done(((bf16[1,48,1536]{2,1,0:T(8,128)(2,1)}), bf16[1,768,1536]{2,1,0:T(8,128)(2,1)}) %all-gather.27.cloned.1.call-update) | async-done | bytes 2359312 | tf_op jit(solution)/shard_map/all_gather | solution.py:81
  236.9 44.2 %all-gather.29.cloned.1.call-done = bf16[1,1536,768]{1,2,0:T(8,128)(2,1)} async-done(((bf16[1,1536,48]{1,2,0:T(8,128)(2,1)}), bf16[1,1536,768]{1,2,0:T(8,128)(2,1)}) %all-gather.29.cloned.1.call-update) | async-done | bytes 2359312 | tf_op jit(solution)/shard_map/all_gather | solution.py:83
  281.1 4.1 fusion.6
  286.7 5.0 all-to-all-start.1
  291.8 26.1 %all-gather.9 = bf16[1,4,768]{1,0,2:T(2,128)(2,1)S(1)} all-gather(bf16[1,4,48]{1,0,2:T(2,128)(2,1)S(1)} %copy.306), channel_id=11, replica_groups=mesh['shard'=16,'context'=4,'tensor'=2] {'shard'}, dimensions={2}, use_global_device_ids=true | all-gather | bytes 6528 | tf_op jit(solution)/shard_map/all_gather | solution.py:85
  318.5 22.5 %all-gather.8 = bf16[1,2,768]{1,0,2:T(2,128)(2,1)S(1)} all-gather(bf16[1,2,48]{1,0,2:T(2,128)(2,1)S(1)} %copy.305), channel_id=10, replica_groups=mesh['shard'=16,'context'=4,'tensor'=2] {'shard'}, dimensions={2}, use_global_device_ids=true | all-gather | bytes 3264 | tf_op jit(solution)/shard_map/all_gather | solution.py:84
  341.4 22.2 %all-gather.11 = bf16[1,2,6,64]{2,1,0,3:T(2,128)(2,1)S(1)} all-gather(bf16[1,2,6,4]{2,1,0,3:T(2,128)(2,1)S(1)} %copy.307), channel_id=13, replica_groups=mesh['shard'=16,'context'=4,'tensor'=2] {'shard'}, dimensions={3}, use_global_device_ids=true | all-gather | bytes 1632 | tf_op jit(solution)/shard_map/all_gather | solution.py:79
  365.0 4.6 slice_reduce_fusion.2
  369.6 11.2 slice_reduce_fusion
  386.3 15.3 %all-gather.12 = bf16[1,2,512,384]{3,2,0,1:T(8,128)(2,1)} all-gather(bf16[1,2,128,384]{3,2,0,1:T(8,128)(2,1)S(1)} %slice.236), channel_id=14, replica_groups=mesh['shard'=16,'context'=4,'tensor'=2] {'context'}, dimensions={2}, use_global_device_ids=true | all-gather | bytes 983040 | tf_op jit(solution)/shard_map/all_gather | solution.py:109
  406.2 14.1 all_gather.86
  431.4 21.5 %all-gather.14 = bf16[1,24,64]{1,0,2:T(2,128)(2,1)S(1)} all-gather(bf16[1,24,4]{1,0,2:T(2,128)(2,1)S(1)} %copy.308), channel_id=16, replica_groups=mesh['shard'=16,'context'=4,'tensor'=2] {'shard'}, dimensions={2}, use_global_device_ids=true | all-gather | bytes 3264 | tf_op jit(solution)/shard_map/all_gather | solution.py:82
  456.2 47.1 %all-gather.33.cloned.1.call-done = bf16[1,768,1536]{2,1,0:T(8,128)(2,1)} async-done(((bf16[1,48,1536]{2,1,0:T(8,128)(2,1)}), bf16[1,768,1536]{2,1,0:T(8,128)(2,1)}) %all-gather.33.cloned.1.call-update) | async-done | bytes 2359312 | tf_op jit(solution)/shard_map/all_gather | solution.py:81
  507.1 43.8 %all-gather.35.cloned.1.call-done = bf16[1,1536,768]{1,2,0:T(8,128)(2,1)} async-done(((bf16[1,1536,48]{1,2,0:T(8,128)(2,1)}), bf16[1,1536,768]{1,2,0:T(8,128)(2,1)}) %all-gather.35.cloned.1.call-update) | async-done | bytes 2359312 | tf_op jit(solution)/shard_map/all_gather | solution.py:83
  550.8 4.5 fusion.153
  557.8 4.1 fusion.3
  562.0 25.5 %all-gather.16 = bf16[1,384,768]{1,2,0:T(8,128)(2,1)} all-gather(bf16[1,384,48]{1,2,0:T(8,128)(2,1)} %get-tuple-element.107), channel_id=18, replica_groups=mesh['shard'=16,'context'=4,'tensor'=2] {'shard'}, dimensions={2}, use_global_device_ids=true | all-gather | bytes 626688 | tf_op jit(solution)/shard_map/all_gather | solution.py:188
  590.0 20.4 %all-reduce.34.cloned.1.call-done = f32[2,128,768]{2,1,0:T(8,128)} async-done(((f32[2,128,768]{2,1,0:T(8,128)}), f32[2,128,768]{2,1,0:T(8,128)}) %all-reduce.34.cloned.1.call-update) | async-done | bytes 786448 | tf_op jit(solution)/shard_map/psum | solution.py:144
  627.0 3.8 convolution_convert_fusion.2
  638.5 12.4 reduce-scatter.21.cloned.1.call-done
  650.9 24.8 %reduce-scatter.23.cloned.1.call-done = bf16[2,128,384]{2,1,0:T(8,128)(2,1)} async-done(((bf16[2,512,384]{2,1,0:T(8,128)(2,1)}), bf16[2,128,384]{2,1,0:T(8,128)(2,1)}) %reduce-scatter.23.cloned.1.call-update) | async-done | bytes 196624 | tf_op jit(solution)/shard_map/reduce_scatter | solution.py:261
  679.0 23.9 %all-reduce.38.cloned.1.call-done = bf16[2,128,768]{2,1,0:T(8,128)(2,1)} async-done(((bf16[2,128,768]{2,1,0:T(8,128)(2,1)}), bf16[2,128,768]{2,1,0:T(8,128)(2,1)}) %all-reduce.38.cloned.1.call-update) | async-done | bytes 393232 | tf_op jit(solution)/shard_map/psum | solution.py:275
  711.7 27.2 %all-gather.17 = bf16[1,384,768]{1,2,0:T(8,128)(2,1)} all-gather(bf16[1,384,48]{1,2,0:T(8,128)(2,1)} %get-tuple-element.104), channel_id=19, replica_groups=mesh['shard'=16,'context'=4,'tensor'=2] {'shard'}, dimensions={2}, use_global_device_ids=true | all-gather | bytes 626688 | tf_op jit(solution)/shard_map/all_gather | solution.py:188
  756.2 3.8 convolution_convert_fusion
  766.1 12.3 reduce-scatter.25.cloned.1.call-done
  778.4 24.6 %reduce-scatter.27.cloned.1.call-done = bf16[2,128,384]{2,1,0:T(8,128)(2,1)} async-done(((bf16[2,512,384]{2,1,0:T(8,128)(2,1)}), bf16[2,128,384]{2,1,0:T(8,128)(2,1)}) %reduce-scatter.27.cloned.1.call-update) | async-done | bytes 196624 | tf_op jit(solution)/shard_map/reduce_scatter | solution.py:261
  814.5 5.3 copy.254
  821.8 5.2 copy.252
  832.3 3.9 bitcast_convert_fusion
  850.2 75.5 %all-reduce.12 = (bf16[2,6,64]{1,0,2:T(2,128)(2,1)S(1)}, bf16[2,6,64]{1,0,2:T(2,128)(2,1)S(1)}, bf16[24,64]{1,0:T(8,128)(2,1)S(1)}, bf16[24,64]{1,0:T(8,128)(2,1...) all-reduce(bf16[2,6,64]{1,0,2:T(2,128)(2,1)S(1)} %copy.259, ...), channel_id=27, replica_groups=mesh['shard'=16,'context'=4,'tensor'=2] {'shard'}, use_global_device_ids=true, to_apply=%region_44.45.clone | all-reduce | flops 13824 | bytes 55296
  930.9 51.5 %reduce-scatter.37.cloned.1.call-done = bf16[384,48]{0,1:T(8,128)(2,1)} async-done(((bf16[384,768]{0,1:T(8,128)(2,1)}), bf16[384,48]{0,1:T(8,128)(2,1)}) %reduce-scatter.37.cloned.1.call-update) | async-done | bytes 36880
  982.4 111.1 %all-reduce.44.cloned.1.call-done = (bf16[3,768,384]{2,0,1:T(4,128)(2,1)}, bf16[3,768,384]{2,0,1:T(4,128)(2,1)}) async-done(((bf16[3,768,384]{2,0,1:T(4,128)(2,1)}, bf16[3,768,384]{2,0,1:T(4,128)(2,1)}), (bf16[3,768,384]{2,0,1:T(4,128)(2,1)}, bf16[3,768,384]{2,0,1:T(4,128)(2,1)})) %all-reduce.44.cloned.1.call-update) | async-done | bytes 3538960
  1096.7 75.1 %reduce-scatter.31.cloned.1.call-done = bf16[48,1536]{1,0:T(8,128)(2,1)} async-done(((bf16[768,1536]{1,0:T(8,128)(2,1)}), bf16[48,1536]{1,0:T(8,128)(2,1)}) %reduce-scatter.31.cloned.1.call-update) | async-done | bytes 147472 | tf_op jit(solution)/shard_map/reduce_scatter | solution.py:311
  1171.8 77.9 %reduce-scatter.35.cloned.1.call-done = bf16[1536,48]{0,1:T(8,128)(2,1)} async-done(((bf16[1536,768]{0,1:T(8,128)(2,1)}), bf16[1536,48]{0,1:T(8,128)(2,1)}) %reduce-scatter.35.cloned.1.call-update) | async-done | bytes 147472 | tf_op jit(solution)/shard_map/reduce_scatter | solution.py:323
  1249.7 77.7 %reduce-scatter.29.cloned.1.call-done = bf16[48,1536]{1,0:T(8,128)(2,1)} async-done(((bf16[768,1536]{1,0:T(8,128)(2,1)}), bf16[48,1536]{1,0:T(8,128)(2,1)}) %reduce-scatter.29.cloned.1.call-update) | async-done | bytes 147472 | tf_op jit(solution)/shard_map/reduce_scatter | solution.py:311
  1327.4 77.9 %reduce-scatter.33.cloned.1.call-done = bf16[1536,48]{0,1:T(8,128)(2,1)} async-done(((bf16[1536,768]{0,1:T(8,128)(2,1)}), bf16[1536,48]{0,1:T(8,128)(2,1)}) %reduce-scatter.33.cloned.1.call-update) | async-done | bytes 147472 | tf_op jit(solution)/shard_map/reduce_scatter | solution.py:323
  1406.5 43.3 %all-reduce.46.cloned.1.call-done = (bf16[1,2,6,4]{2,3,1,0:T(4,128)(2,1)}, bf16[1,2,6,4]{2,3,1,0:T(4,128)(2,1)}, bf16[1,384,48]{1,2,0:T(8,128)(2,1)}, bf16[1,384...) async-done(((bf16[1,2,6,4]{2,3,1,0:T(4,128)(2,1)}, ...) | async-done | bytes 75472 | tf_op jit(solution)/shard_map/psum | solution.py:298
  1456.4 42.9 %all-reduce.48.cloned.1.call-done = (bf16[1,3,48,384]{3,1,2,0:T(4,128)(2,1)}, bf16[1,3,48,384]{3,1,2,0:T(4,128)(2,1)}, bf16[1,48,1536]{2,1,0:T(8,128)(2,1)}, bf1...) async-done(((bf16[1,3,48,384]{3,1,2,0:T(4,128)(2,1)}, bf16[1,3,48,384]{3,1,2,0:T(4,128)(2,1)}, bf16[1,48,1536]{2,1,0:T(8,128)(2,1)}, ...) | async-done | bytes 811024 | tf_op jit(solution)/shard_map/psum | solution.py:292
  (427 shorter events, 178.1 us)
Async XLA Ops:
  7.2 12.2 copy-start.79
  7.2 112.7 %all-gather.25.cloned.1.call-start = ((), (), s32[]{:S(2)}) async-start(), calls=%async_computation.28 | async-start | bytes 1880064 | tf_op jit(solution)/shard_map/all_gather | solution.py:78
  8.9 38.5 %copy-start.82 = (bf16[2,2,48]{2,1,0:T(2,128)(2,1)S(1)}, bf16[2,2,48]{2,1,0:T(2,128)(2,1)}, u32[]{:S(2)}) copy-start(bf16[2,2,48]{2,1,0:T(2,128)(2,1)} %param.19) | copy-start | bytes 1156
  11.2 59.3 %copy-start.87 = (s32[2,128]{1,0:T(2,128)S(1)}, s32[2,128]{1,0:T(2,128)}, u32[]{:S(2)}) copy-start(s32[2,128]{1,0:T(2,128)} %param.12) | copy-start | bytes 3076
  11.2 59.3 %copy-start.74 = (bf16[2,2,6,4]{2,3,1,0:T(4,128)(2,1)S(1)}, bf16[2,2,6,4]{2,3,1,0:T(4,128)(2,1)}, u32[]{:S(2)}) copy-start(bf16[2,2,6,4]{2,3,1,0:T(4,128)(2,1)} %param.14) | copy-start | bytes 580
  11.2 81.9 %copy-start = (f32[2,128,768]{2,1,0:T(8,128)S(1)}, f32[2,128,768]{2,1,0:T(8,128)}, u32[]{:S(2)}) copy-start(f32[2,128,768]{2,1,0:T(8,128)} %param.11) | copy-start | bytes 2359300
  11.2 146.9 %all-to-all-start = ((bf16[384,16,48]{0,2,1:T(8,128)(2,1)}), bf16[384,16,48]{0,2,1:T(8,128)(2,1)}, u32[]{:S(2)}, u32[]{:S(2)}) async-start(bf16[384,16,48]{0,2,1:T(8,128)(2,1)} %tile.17), calls=%async_computation | async-start | bytes 1179648 | tf_op jit(solution)/shard_map/all_to_all | solution.py:16
  19.3 165.9 %all-reduce.28.cloned.1.call-start = ((), (), s32[]{:S(2)}) async-start(), calls=%async_computation.12 | async-start | bytes 1572864 | tf_op jit(solution)/shard_map/psum | solution.py:134
  92.9 61.5 %copy-start.47 = (f32[6,64]{1,0:T(8,128)}, f32[6,64]{1,0:T(8,128)S(1)}, u32[]{:S(2)}) copy-start(f32[6,64]{1,0:T(8,128)S(1)} %copy.221) | copy-start | bytes 4612
  103.7 18.5 %copy-start.43 = (f32[2,128]{1,0:T(2,128)}, f32[2,128]{1,0:T(2,128)S(1)}, u32[]{:S(2)}) copy-start(f32[2,128]{1,0:T(2,128)S(1)} %broadcast_multiply_fusion.11) | copy-start | bytes 3076
  108.5 13.7 copy-start.50
  108.8 47.5 %copy-start.16 = (pred[2,128,512]{2,1,0:T(8,128)(4,1)}, pred[2,128,512]{2,1,0:T(8,128)(4,1)S(1)}, u32[]{:S(2)}) copy-start(pred[2,128,512]{2,1,0:T(8,128)(4,1)S(1)} %compare_and_fusion) | copy-start | bytes 393220
  119.8 113.4 %copy-start.58 = (f32[768]{0:T(1024)}, f32[768]{0:T(1024)S(1)}, u32[]{:S(2)}) copy-start(f32[768]{0:T(1024)S(1)} %get-tuple-element.49) | copy-start | bytes 9220
  138.4 16.0 %copy-start.6 = (bf16[1,2,512,384]{2,3,1,0:T(8,128)(2,1)}, bf16[1,2,512,384]{2,3,1,0:T(8,128)(2,1)S(1)}, u32[]{:S(2)}) copy-start(bf16[1,2,512,384]{2,3,1,0:T(8,128)(2,1)S(1)} %copy.222) | copy-start | bytes 2359300
  160.6 72.7 %all-gather.27.cloned.1.call-start = ((), (), s32[]{:S(2)}) async-start(), calls=%async_computation.29 | async-start | bytes 2506752 | tf_op jit(solution)/shard_map/all_gather | solution.py:81
  161.4 119.8 %all-gather.29.cloned.1.call-start = ((), (), s32[]{:S(2)}) async-start(), calls=%async_computation.30 | async-start | bytes 2506752 | tf_op jit(solution)/shard_map/all_gather | solution.py:83
  162.2 218.6 %all-reduce.30.cloned.1.call-start = ((), (), s32[]{:S(2)}) async-start(), calls=%async_computation.13 | async-start | bytes 1572864 | tf_op jit(solution)/shard_map/psum | solution.py:144
  186.5 50.4 %copy-start.53 = (f32[2,128]{1,0:T(2,128)}, f32[2,128]{1,0:T(2,128)S(1)}, u32[]{:S(2)}) copy-start(f32[2,128]{1,0:T(2,128)S(1)} %broadcast_multiply_fusion.10) | copy-start | bytes 3076
  186.8 50.1 %copy-start.60 = (f32[2,128]{1,0:T(2,128)}, f32[2,128]{1,0:T(2,128)S(1)}, u32[]{:S(2)}) copy-start(f32[2,128]{1,0:T(2,128)S(1)} %add_rsqrt_fusion.2) | copy-start | bytes 3076
  285.2 6.5 copy-start.77
  285.2 33.1 %copy-start.81 = (bf16[1,2,48]{2,1,0:T(2,128)(2,1)S(1)}, bf16[1,2,48]{2,1,0:T(2,128)(2,1)}, u32[]{:S(2)}) copy-start(bf16[1,2,48]{2,1,0:T(2,128)(2,1)} %get-tuple-element.118) | copy-start | bytes 580
  285.2 97.1 %all-gather.31.cloned.1.call-start = ((), (), s32[]{:S(2)}) async-start(), calls=%async_computation.31 | async-start | bytes 1880064 | tf_op jit(solution)/shard_map/all_gather | solution.py:78
  286.7 140.7 %all-to-all-start.1 = ((bf16[384,16,48]{0,2,1:T(8,128)(2,1)}), bf16[384,16,48]{0,2,1:T(8,128)(2,1)}, u32[]{:S(2)}, u32[]{:S(2)}) async-start(bf16[384,16,48]{0,2,1:T(8,128)(2,1)} %tile.19), calls=%async_computation.1 | async-start | bytes 1179648 | tf_op jit(solution)/shard_map/all_to_all | solution.py:16
  291.7 161.9 %all-reduce.32.cloned.1.call-start = ((), (), s32[]{:S(2)}) async-start(), calls=%async_computation.14 | async-start | bytes 1572864 | tf_op jit(solution)/shard_map/psum | solution.py:134
  403.0 19.7 %copy-start.7 = (bf16[1,2,512,384]{2,3,1,0:T(8,128)(2,1)}, bf16[1,2,512,384]{2,3,1,0:T(8,128)(2,1)S(1)}, u32[]{:S(2)}) copy-start(bf16[1,2,512,384]{2,3,1,0:T(8,128)(2,1)S(1)} %copy.235) | copy-start | bytes 2359300
  427.3 26.3 %copy-start.25 = (bf16[2,6,64,128]{3,2,1,0:T(8,128)(2,1)}, bf16[2,6,64,128]{3,2,1,0:T(8,128)(2,1)S(1)}, u32[]{:S(2)}) copy-start(bf16[2,6,64,128]{3,2,1,0:T(8,128)(2,1)S(1)} %convolution_convert_fusion.4) | copy-start | bytes 589828
  429.8 73.6 %all-gather.33.cloned.1.call-start = ((), (), s32[]{:S(2)}) async-start(), calls=%async_computation.32 | async-start | bytes 2506752 | tf_op jit(solution)/shard_map/all_gather | solution.py:81
  430.6 120.3 %all-gather.35.cloned.1.call-start = ((), (), s32[]{:S(2)}) async-start(), calls=%async_computation.33 | async-start | bytes 2506752 | tf_op jit(solution)/shard_map/all_gather | solution.py:83
  431.3 156.2 %all-reduce.36.cloned.1.call-start = ((), (), s32[]{:S(2)}) async-start(), calls=%async_computation.16 | async-start | bytes 786432 | tf_op jit(solution)/shard_map/psum | solution.py:222
  557.7 52.7 %all-reduce.34.cloned.1.call-start = ((), (), s32[]{:S(2)}) async-start(), calls=%async_computation.15 | async-start | bytes 1572864 | tf_op jit(solution)/shard_map/psum | solution.py:144
  561.9 89.0 %reduce-scatter.21.cloned.1.call-start = ((), (), s32[]{:S(2)}) async-start(), calls=%async_computation.17 | async-start | bytes 983040 | tf_op jit(solution)/shard_map/reduce_scatter | solution.py:258
  626.9 48.8 %reduce-scatter.23.cloned.1.call-start = ((), (), s32[]{:S(2)}) async-start(), calls=%async_computation.18 | async-start | bytes 983040 | tf_op jit(solution)/shard_map/reduce_scatter | solution.py:261
  633.1 69.9 %all-reduce.38.cloned.1.call-start = ((), (), s32[]{:S(2)}) async-start(), calls=%async_computation.19 | async-start | bytes 786432 | tf_op jit(solution)/shard_map/psum | solution.py:275
  679.0 59.9 %all-reduce.40.cloned.1.call-start = ((), (), s32[]{:S(2)}) async-start(), calls=%async_computation.20 | async-start | bytes 786432 | tf_op jit(solution)/shard_map/psum | solution.py:222
  711.7 66.7 %reduce-scatter.25.cloned.1.call-start = ((), (), s32[]{:S(2)}) async-start(), calls=%async_computation.21 | async-start | bytes 983040 | tf_op jit(solution)/shard_map/reduce_scatter | solution.py:258
  756.1 46.9 %reduce-scatter.27.cloned.1.call-start = ((), (), s32[]{:S(2)}) async-start(), calls=%async_computation.22 | async-start | bytes 983040 | tf_op jit(solution)/shard_map/reduce_scatter | solution.py:261
  762.3 85.3 %all-reduce.42.cloned.1.call-start = ((), (), s32[]{:S(2)}) async-start(), calls=%async_computation.23 | async-start | bytes 786432 | tf_op jit(solution)/shard_map/psum | solution.py:275
  806.4 124.4 %reduce-scatter.39.cloned.1.call-start = ((), (), s32[]{:S(2)}) async-start(), calls=%async_computation.35 | async-start | bytes 626688
  808.9 173.4 %reduce-scatter.37.cloned.1.call-start = ((), (), s32[]{:S(2)}) async-start(), calls=%async_computation.34 | async-start | bytes 626688
  811.4 282.1 %all-reduce.44.cloned.1.call-start = ((), (), s32[]{:S(2)}) async-start(), calls=%async_computation.36 | async-start | bytes 9437184
  827.0 344.8 %reduce-scatter.31.cloned.1.call-start = ((), (), s32[]{:S(2)}) async-start(), calls=%async_computation.25 | async-start | bytes 2506752 | tf_op jit(solution)/shard_map/reduce_scatter | solution.py:311
  831.2 418.4 %reduce-scatter.35.cloned.1.call-start = ((), (), s32[]{:S(2)}) async-start(), calls=%async_computation.27 | async-start | bytes 2506752 | tf_op jit(solution)/shard_map/reduce_scatter | solution.py:323
  836.2 491.1 %reduce-scatter.29.cloned.1.call-start = ((), (), s32[]{:S(2)}) async-start(), calls=%async_computation.24 | async-start | bytes 2506752 | tf_op jit(solution)/shard_map/reduce_scatter | solution.py:311
  839.7 565.6 %reduce-scatter.33.cloned.1.call-start = ((), (), s32[]{:S(2)}) async-start(), calls=%async_computation.26 | async-start | bytes 2506752 | tf_op jit(solution)/shard_map/reduce_scatter | solution.py:323
  843.9 605.9 %all-reduce.46.cloned.1.call-start = ((), (), s32[]{:S(2)}) async-start(), calls=%async_computation.37 | async-start | bytes 165888 | tf_op jit(solution)/shard_map/psum | solution.py:298
  847.3 558.0 %copy-start.4 = (f32[2,128,768]{2,1,0:T(8,128)S(1)}, f32[2,128,768]{2,1,0:T(8,128)}, u32[]{:S(2)}) copy-start(f32[2,128,768]{2,1,0:T(8,128)} %copy-done.3) | copy-start | bytes 2359300
  847.6 557.7 %copy-start.15 = (bf16[2,128,768]{2,1,0:T(8,128)(2,1)S(1)}, bf16[2,128,768]{2,1,0:T(8,128)(2,1)}, u32[]{:S(2)}) copy-start(bf16[2,128,768]{2,1,0:T(8,128)(2,1)} %all-reduce.42.cloned.1.call-done) | copy-start | bytes 1179652
  982.3 516.9 %all-reduce.48.cloned.1.call-start = ((), (), s32[]{:S(2)}) async-start(), calls=%async_computation.38 | async-start | bytes 1769472 | tf_op jit(solution)/shard_map/psum | solution.py:292
  (72 other events, 195.4 us)
Sparse Core Ops, SparseCore 0:
  10.8 48.6 all-gather.24
  160.7 22.3 all-reduce.27
  186.0 47.1 all-gather.26
  236.0 45.0 all-gather.28
  285.4 24.0 all-reduce.29
  312.0 45.8 all-gather.30
  429.9 23.2 all-reduce.31
  456.2 47.1 all-gather.32
  505.7 45.0 all-gather.34
  557.9 23.2 all-reduce.35
  584.2 26.1 all-reduce.33
  627.1 23.7 reduce-scatter.20
  653.4 22.2 reduce-scatter.22
  679.1 23.8 all-reduce.37
  711.8 25.3 all-reduce.39
  756.3 22.1 reduce-scatter.24
  780.8 22.2 reduce-scatter.26
  806.5 23.8 all-reduce.41
  834.2 73.2 reduce-scatter.38
  911.1 71.1 reduce-scatter.36
  985.8 107.6 all-reduce.43
  1097.1 74.6 reduce-scatter.30
  1175.5 74.1 reduce-scatter.34
  1253.2 74.1 reduce-scatter.28
  1331.0 74.2 reduce-scatter.32
  1409.6 40.1 all-reduce.45
  1453.0 46.2 all-reduce.47
